TPU v7x, 32 devices: a whole 2x2x4 slice. The times are simulated.
32 devices in a mesh: seq: 16 (over z, y, x), dp: 2 (over core).
Axes of the slice: x: 2, y: 2, z: 4, core: 2. Of those that a mesh axis runs over, the one named last changes fastest.
Arguments:
- query_rows: bfloat16 [2, 2048, 1024], P('dp', 'seq'), may hold values from -6 to 6
- key_rows: bfloat16 [2, 2048, 1024], P('dp', 'seq'), may hold values from -6 to 6
- value_rows: bfloat16 [2, 2048, 1024], P('dp', 'seq'), may hold values from -6 to 6
- out_grad: bfloat16 [2, 2048, 1024], P('dp', 'seq'), may hold values from -6 to 6
- query_gain: float32 [1024], replicated, may hold values from 0.1 to 1.9
- key_gain: float32 [1024], replicated, may hold values from 0.1 to 1.9
Outputs:
- query_grad: bfloat16 [2, 2048, 1024], P('dp', 'seq')
- key_grad: bfloat16 [2, 2048, 1024], P('dp', 'seq')
- value_grad: bfloat16 [2, 2048, 1024], P('dp', 'seq')
- query_gain_grad: float32 [1024], replicated
- key_gain_grad: float32 [1024], replicated
All inputs are finite; a program needn't handle non-finite values.
Results may differ from a plain program's by a relative error of at most 0.0065.
Values sent between devices are 32-bit elements; how exact they have to be, the bound alone decides.
A program may use at most 64 MiB of HBM per device.

v0:
```python
import math

import jax
import jax.numpy as jnp
from jax import lax
from jax.sharding import PartitionSpec as P

HEADS = 16
HEAD_DIM = 64


def prefix(part, axis, combine, identity, reverse):
    count = lax.axis_size(axis)
    place = lax.axis_index(axis)
    ahead = count - 1 - place if reverse else place
    gathered = lax.all_gather(part, axis)
    state = jnp.zeros_like(part) + jnp.asarray(identity, part.dtype)

    def one(turn, state):
        source = count - 1 - turn if reverse else turn
        return combine(state, lax.dynamic_index_in_dim(gathered, source, 0, False))

    return lax.fori_loop(0, ahead, one, state)


def add_one(earlier, later):
    return earlier + later


def local(query_rows, key_rows, value_rows, out_grad, query_gain, key_gain):
    rows = query_rows.shape[1]
    width = query_rows.shape[2]
    seq_len = rows * lax.axis_size("seq")
    score_scale = 1.0 / math.sqrt(HEAD_DIM * seq_len)
    factor = 1.0 / math.sqrt(seq_len * lax.axis_size("dp"))
    gain_q = query_gain.reshape(HEADS, HEAD_DIM)
    gain_k = key_gain.reshape(HEADS, HEAD_DIM)
    queries = query_rows[0].reshape(rows, HEADS, HEAD_DIM)
    keys_in = key_rows[0].reshape(rows, HEADS, HEAD_DIM)
    value_inputs = value_rows[0].reshape(rows, HEADS, HEAD_DIM)
    grads = out_grad[0].reshape(rows, HEADS, HEAD_DIM)
    gained_q = (queries.astype(jnp.float32) * gain_q).astype(jnp.bfloat16)
    gained_k = (keys_in.astype(jnp.float32) * gain_k).astype(jnp.bfloat16)
    flat_shape = (HEADS, HEAD_DIM * HEAD_DIM)
    state_shape = (HEADS, HEAD_DIM, HEAD_DIM)
    local_scores = jnp.einsum(
        "thd,the->hde", gained_k, value_inputs, preferred_element_type=jnp.float32
    ).reshape(flat_shape)
    own_b = jnp.einsum("thd,the->hde", gained_q, grads, preferred_element_type=jnp.float32).reshape(
        flat_shape
    )
    zeros = jnp.zeros_like(local_scores)
    prefix_a = prefix(local_scores, "seq", add_one, zeros, False)
    suffix_state = prefix(own_b, "seq", add_one, zeros, True)
    prefix_a = prefix_a.astype(jnp.bfloat16).reshape(state_shape)
    suffix_state = suffix_state.astype(jnp.bfloat16).reshape(state_shape)
    row_pos = lax.broadcasted_iota(jnp.int32, (rows, rows), 0)
    col_pos = lax.broadcasted_iota(jnp.int32, (rows, rows), 1)
    causal_masked = row_pos >= col_pos
    pairwise_grad = jnp.einsum(
        "the,she->hts", grads, value_inputs, preferred_element_type=jnp.float32
    )
    pairwise_grad = jnp.where(causal_masked, pairwise_grad, 0.0).astype(jnp.bfloat16)
    pair_score = jnp.einsum("thd,shd->hts", gained_q, gained_k, preferred_element_type=jnp.float32)
    pair_score = jnp.where(causal_masked, pair_score, 0.0).astype(jnp.bfloat16)
    dq_gained = score_scale * (
        jnp.einsum("hts,shd->thd", pairwise_grad, gained_k, preferred_element_type=jnp.float32)
        + jnp.einsum("the,hde->thd", grads, prefix_a, preferred_element_type=jnp.float32)
    )
    gained_key_grad = score_scale * (
        jnp.einsum("hts,thd->shd", pairwise_grad, gained_q, preferred_element_type=jnp.float32)
        + jnp.einsum("she,hde->shd", value_inputs, suffix_state, preferred_element_type=jnp.float32)
    )
    value_part = score_scale * (
        jnp.einsum("hts,the->she", pair_score, grads, preferred_element_type=jnp.float32)
        + jnp.einsum("shd,hde->she", gained_k, suffix_state, preferred_element_type=jnp.float32)
    )
    query_grad = (dq_gained * gain_q).astype(jnp.bfloat16).reshape(1, rows, width)
    key_grad = (gained_key_grad * gain_k).astype(jnp.bfloat16).reshape(1, rows, width)
    value_grad = value_part.astype(jnp.bfloat16).reshape(1, rows, width)
    q_part = jnp.sum(dq_gained * queries.astype(jnp.float32), axis=0).reshape(width)
    k_part = jnp.sum(gained_key_grad * keys_in.astype(jnp.float32), axis=0).reshape(width)
    q_total, k_total = lax.psum((q_part, k_part), ("seq", "dp"))
    return (query_grad, key_grad, value_grad, q_total * factor, k_total * factor)


def solution(mesh):
    in_specs = (
        P("dp", "seq", None),
        P("dp", "seq", None),
        P("dp", "seq", None),
        P("dp", "seq", None),
        P(),
        P(),
    )
    out_specs = (P("dp", "seq", None), P("dp", "seq", None), P("dp", "seq", None), P(), P())
    return jax.shard_map(local, mesh=mesh, in_specs=in_specs, out_specs=out_specs, check_vma=False)
```

profile of v0, /device:TPU:0, one launch (start us, length us, event | category | flops | bytes accessed | tf_op | source)
XLA Modules:
  0.0 243.6 jit_solution(15766306827989951453)
XLA Ops:
  8.1 1.1 copy.33
  9.2 1.1 copy.35
  10.7 0.9 all_gather_reshape.7
  13.4 77.2 %all-gather.5.cloned.1.call-done = f32[16,16,4096]{2,1,0:T(8,128)} async-done(((f32[1,16,4096]{2,1,0:T(8,128)}), f32[16,16,4096]{2,1,0:T(8,128)}) %all-gather.5.cloned.1.call-update) | async-done | bytes 4194320 | tf_op jit(solution)/shard_map/all_gather | solution.py:16
  90.6 15.5 %while.23 = (s32[]{:T(128)}, f32[16,4096]{1,0:T(8,128)S(1)}, s32[]{:T(128)}, f32[16,16,4096]{2,1,0:T(8,128)}, s32[]{:T(128)}, /*index=5*/s32[]{:T(128)}, s32[]{:T(128)}, s32[]{:T(128)}) while((s32[]{:T(128)}, f32[16,4096]{1,0:T(8,128)S(1)}, s32[]{:T(128)}, f32[16,16,4096]{2,1,0:T(8,128)}, s32[]{:T(128)}, /*index=5*/s32[]{:T(128)}, s32[]{:T(128)}, ...), condition=%wide.region_3.4_spmd, body=%wide.region_2.3_spmd.sunk | while | flops 65542 | bytes 786575 | solution.py:23
  90.7 1.0 bitcast_add_fusion.5
  91.7 1.0 bitcast_add_fusion.5
  92.7 1.0 bitcast_add_fusion.5
  93.7 1.0 bitcast_add_fusion.5
  94.8 1.0 bitcast_add_fusion.5
  95.8 1.0 bitcast_add_fusion.5
  96.8 1.0 bitcast_add_fusion.5
  97.9 1.0 bitcast_add_fusion.5
  98.9 1.0 bitcast_add_fusion.5
  99.9 1.0 bitcast_add_fusion.5
  101.0 1.0 bitcast_add_fusion.5
  102.0 1.0 bitcast_add_fusion.5
  103.0 1.0 bitcast_add_fusion.5
  104.0 1.0 bitcast_add_fusion.5
  105.1 1.0 bitcast_add_fusion.5
  106.4 1.7 fusion.7
  110.8 1.2 multiply_convert_fusion
  114.9 66.8 %all-gather.3.cloned.1.call-done = f32[16,16,4096]{2,1,0:T(8,128)} async-done(((f32[1,16,4096]{2,1,0:T(8,128)}), f32[16,16,4096]{2,1,0:T(8,128)}) %all-gather.3.cloned.1.call-update) | async-done | bytes 4194320 | tf_op jit(solution)/shard_map/all_gather | solution.py:16
  183.5 52.7 %all-reduce = (f32[1024]{0:T(1024)S(1)}, f32[1024]{0:T(1024)S(1)}) all-reduce(f32[1024]{0:T(1024)S(1)} %reshape.42, f32[1024]{0:T(1024)S(1)} %reshape.43), channel_id=1, replica_groups=mesh['seq'=16,'dp'=2] {'seq','dp'}, use_global_device_ids=true, to_apply=%region_5.6 | all-reduce | flops 2048 | bytes 16384 | tf_op jit(solution)/shard_map/psum | solution.py:83
  (43 shorter events, 11.1 us)
Async XLA Ops:
  7.2 4.6 %copy-start.3 = (f32[1024]{0:T(1024)S(1)}, f32[1024]{0:T(1024)}, u32[]{:S(2)}) copy-start(f32[1024]{0:T(1024)} %param.15) | copy-start | bytes 12292
  7.2 5.2 %copy-start.1 = (bf16[1,128,1024]{2,1,0:T(8,128)(2,1)S(1)}, bf16[1,128,1024]{2,1,0:T(8,128)(2,1)}, u32[]{:S(2)}) copy-start(bf16[1,128,1024]{2,1,0:T(8,128)(2,1)} %param.12) | copy-start | bytes 786436
  7.2 5.4 %copy-start = (bf16[1,128,1024]{2,1,0:T(8,128)(2,1)S(1)}, bf16[1,128,1024]{2,1,0:T(8,128)(2,1)}, u32[]{:S(2)}) copy-start(bf16[1,128,1024]{2,1,0:T(8,128)(2,1)} %param.11) | copy-start | bytes 786436
  7.2 83.4 %all-gather.5.cloned.1.call-start = ((), (), s32[]{:S(2)}) async-start(), calls=%async_computation.1 | async-start | bytes 4456448 | tf_op jit(solution)/shard_map/all_gather | solution.py:16
  8.0 2.4 copy-start.2
  11.7 170.1 %all-gather.3.cloned.1.call-start = ((), (), s32[]{:S(2)}) async-start(), calls=%async_computation | async-start | bytes 4456448 | tf_op jit(solution)/shard_map/all_gather | solution.py:16
Sparse Core Ops, SparseCore 0:
  11.8 78.7 all-gather.4
  109.4 72.2 all-gather.2
where the time goes:
time: 245 us; the launch traced here: 244 us
  waiting for transfers between devices  144 us (59%)
  blocking collectives  52.7 us (22%)
  other arithmetic  18.8 us (8%)
  between operations  14.2 us (6%)
  local copies, waits for them, and re-layouts  8.97 us (4%)
  matrix products  4.32 us (2%)
    all_gather x2, waiting for transfers between devices, prefix(): gathered = lax.all_gather(part, axis)  144 us
    psum x1, blocking collectives, local(): q_total, k_total = lax.psum((q_part, k_part), ('seq', 'dp'))  52.7 us
    add x15, other arithmetic, add_one(): return earlier + later  15.1 us
  transfers between devices with their start and end apart: 2, of which 2 were waited for; matrix products, arithmetic and copies ran while one was open for 3% of the time, Pallas kernels for 0%

commit v1 on v0

v1 whole, which is shorter than its diff:
```python
import functools
import math

import jax
import jax.numpy as jnp
from jax import lax
from jax.experimental import pallas as pl
from jax.experimental.pallas import tpu as pltpu
from jax.sharding import PartitionSpec as P

HEADS = 16
HEAD_DIM = 64
PLANE = 4
MESH = pl.DeviceIdType.MESH
F32 = jnp.float32
BF16 = jnp.bfloat16
LANES = 2 * HEAD_DIM
PAIRS = HEADS // 2
CHUNKS = PAIRS // PLANE


def dot(a, b, da, db):
    return lax.dot_general(a, b, (((da,), (db,)), ((), ())), preferred_element_type=F32)


def kernel(n, ndp, rows, score_scale, factor, q_h, k_h, v_h, g_h, gain_q, gain_k,
           qo, ko, vo, gqo, gko,
           qx, kx, vx, gx, gq, gk, dqs, dks, dvs,
           own, rx1, zs, zr, exc, tx2, rx2, gtx, grx,
           in_sem, s1, r1, sz, rz, s2, r2, sg, rg):
    nz = n // PLANE
    dists = []
    d = 1
    while d < nz:
        dists.append(d)
        d *= 2
    me = lax.axis_index("seq")
    dp = lax.axis_index("dp")
    z = me // PLANE
    slot = me % PLANE
    x = slot % 2
    y = slot // 2
    fx = 1 - 2 * x
    fy = 2 - 4 * y
    hops = [fx, fy, fx + fy]

    loads = []
    for i, (src, dst) in enumerate(((k_h, kx), (v_h, vx), (q_h, qx), (g_h, gx))):
        cp = pltpu.make_async_copy(src.at[0], dst, in_sem.at[i])
        cp.start()
        loads.append(cp)

    barrier = pltpu.get_barrier_semaphore()

    def greet(**where):
        pl.semaphore_signal(barrier, inc=1, device_id=where, device_id_type=MESH)

    for h in hops:
        greet(seq=me + h)
    for d in dists:
        @pl.when(z + d < nz)
        def _(d=d):
            greet(seq=me + d * PLANE)

        @pl.when(z >= d)
        def _(d=d):
            greet(seq=me - d * PLANE)
    dp_bits = []
    d = 1
    while d < ndp:
        dp_bits.append(d)
        d *= 2
    for d in dp_bits:
        greet(dp=dp + d * (1 - 2 * ((dp // d) % 2)))

    lane = lax.broadcasted_iota(jnp.int32, (1, LANES), 1)
    first = (lane < HEAD_DIM).astype(F32).astype(BF16)
    second = (lane >= HEAD_DIM).astype(F32).astype(BF16)
    left = lax.broadcasted_iota(jnp.int32, (HEAD_DIM, LANES), 1) < HEAD_DIM

    def stack(t):
        return jnp.concatenate([t * first, t * second], axis=0)

    def cols(pair):
        return pl.ds(pair * LANES, LANES)

    def fold(full):
        return jnp.where(left, full[:HEAD_DIM], full[HEAD_DIM:])

    def copy1(c, h, hop):
        return pltpu.make_async_remote_copy(
            src_ref=own.at[c, slot + hop], dst_ref=rx1.at[c, slot],
            send_sem=s1.at[c, h], recv_sem=r1.at[c, h],
            device_id={"seq": me + hop}, device_id_type=MESH)

    def copy2(c, h, hop):
        return pltpu.make_async_remote_copy(
            src_ref=tx2.at[c, slot + hop], dst_ref=rx2.at[c, slot],
            send_sem=s2.at[c, h], recv_sem=r2.at[c, h],
            device_id={"seq": me + hop}, device_id_type=MESH)

    def copyz(c, s, ab):
        to = me + dists[s] * PLANE if ab == 0 else me - dists[s] * PLANE
        return pltpu.make_async_remote_copy(
            src_ref=zs.at[s, c, ab], dst_ref=zr.at[s, c, ab],
            send_sem=sz.at[s, c, ab], recv_sem=rz.at[s, c, ab],
            device_id={"seq": to}, device_id_type=MESH)

    def sends(s, ab):
        return z + dists[s] < nz if ab == 0 else z >= dists[s]

    def takes(s, ab):
        return z >= dists[s] if ab == 0 else z + dists[s] < nz

    def own_states(c):
        for p in range(PLANE):
            pair = p * CHUNKS + c
            gkp = (kx[:, cols(pair)].astype(F32) * gain_k[pair:pair + 1, :]).astype(BF16)
            gk[:, cols(pair)] = gkp
            own[c, p, 0] = fold(dot(gkp, vx[:, cols(pair)], 0, 0))
        if c == 0:
            loads[2].wait()
            loads[3].wait()
        for p in range(PLANE):
            pair = p * CHUNKS + c
            gqp = (qx[:, cols(pair)].astype(F32) * gain_q[pair:pair + 1, :]).astype(BF16)
            gq[:, cols(pair)] = gqp
            own[c, p, 1] = fold(dot(gqp, gx[:, cols(pair)], 0, 0))

    loads[0].wait()
    loads[1].wait()
    for c in range(CHUNKS):
        own_states(c)
        if c == 0:
            count = len(hops) + len(dp_bits)
            for d in dists:
                count = count + (z + d < nz).astype(jnp.int32) + (z >= d).astype(jnp.int32)
            pl.semaphore_wait(barrier, count)
        for h in (2, 0, 1):
            copy1(c, h, hops[h]).start()
        rx1[c, slot] = own[c, slot]

    row = lax.broadcasted_iota(jnp.int32, (rows, 2 * rows), 0)
    col = lax.broadcasted_iota(jnp.int32, (rows, 2 * rows), 1) % rows
    low = row >= col
    high = col >= row

    def intra(pair):
        sl = cols(pair)
        gv, vv, qv, kv = gx[:, sl], vx[:, sl], gq[:, sl], gk[:, sl]
        gs, qs = stack(gv), stack(qv)
        pg = jnp.where(low, dot(gv, stack(vv), 1, 1), 0.0).astype(BF16)
        dqs[:, sl] = dot(pg, stack(kv), 1, 0)
        pgt = jnp.where(high, dot(vv, gs, 1, 1), 0.0).astype(BF16)
        dks[:, sl] = dot(pgt, qs, 1, 0)
        pst = jnp.where(high, dot(kv, qs, 1, 1), 0.0).astype(BF16)
        dvs[:, sl] = dot(pst, gs, 1, 0)

    for pair in range(PAIRS):
        intra(pair)

    for c in range(CHUNKS):
        for h in range(3):
            copy1(c, h, hops[h]).wait_recv()
        zs[0, c] = (rx1[c, 0] + rx1[c, 1]) + (rx1[c, 2] + rx1[c, 3])
        exc[c] = jnp.zeros_like(exc[c])
        for ab in range(2):
            if dists:
                @pl.when(sends(0, ab))
                def _():
                    copyz(c, 0, ab).start()

    for s in range(len(dists)):
        for c in range(CHUNKS):
            for ab in range(2):
                @pl.when(takes(s, ab))
                def _():
                    copyz(c, s, ab).wait_recv()
                    got = zr[s, c, ab]
                    exc[c, ab] = exc[c, ab] + got
                    if s + 1 < len(dists):
                        zs[s + 1, c, ab] = zs[s, c, ab] + got
                if s + 1 < len(dists):
                    @pl.when(jnp.logical_not(takes(s, ab)))
                    def _():
                        zs[s + 1, c, ab] = zs[s, c, ab]

                    @pl.when(sends(s + 1, ab))
                    def _():
                        copyz(c, s + 1, ab).start()

    for c in range(CHUNKS):
        run = exc[c, 0]
        for p in range(PLANE):
            tx2[c, p, 0] = run
            if p + 1 < PLANE:
                run = run + rx1[c, p, 0]
        run = exc[c, 1]
        for p in reversed(range(PLANE)):
            tx2[c, p, 1] = run
            if p > 0:
                run = run + rx1[c, p, 1]
        for h in (2, 0, 1):
            copy2(c, h, hops[h]).start()
        rx2[c, slot] = tx2[c, slot]

    for c in range(CHUNKS):
        for h in range(3):
            copy2(c, h, hops[h]).wait_recv()
        for p in range(PLANE):
            pair = p * CHUNKS + c
            sl = cols(pair)
            sa = stack(rx2[c, p, 0].astype(BF16))
            sb = stack(rx2[c, p, 1].astype(BF16))
            dq = score_scale * (dqs[:, sl] + dot(gx[:, sl], sa, 1, 1))
            dk = score_scale * (dks[:, sl] + dot(vx[:, sl], sb, 1, 1))
            dv = score_scale * (dvs[:, sl] + dot(gk[:, sl], sb, 1, 0))
            qo[0, :, sl] = (dq * gain_q[pair:pair + 1, :]).astype(BF16)
            ko[0, :, sl] = (dk * gain_k[pair:pair + 1, :]).astype(BF16)
            vo[0, :, sl] = dv.astype(BF16)
            gtx[0, 0, pair:pair + 1, :] = jnp.sum(dq * qx[:, sl].astype(F32), axis=0, keepdims=True)
            gtx[0, 1, pair:pair + 1, :] = jnp.sum(dk * kx[:, sl].astype(F32), axis=0, keepdims=True)

    partners = [{"dp": dp + d * (1 - 2 * ((dp // d) % 2))} for d in dp_bits]
    d = 1
    while d < n:
        partners.append({"seq": me + d * (1 - 2 * ((me // d) % 2))})
        d *= 2

    def copyg(i):
        return pltpu.make_async_remote_copy(
            src_ref=gtx.at[i], dst_ref=grx.at[i], send_sem=sg.at[i], recv_sem=rg.at[i],
            device_id=partners[i], device_id_type=MESH)

    for i in range(len(partners)):
        copyg(i).start()
        copyg(i).wait_recv()
        gtx[i + 1] = gtx[i] + grx[i]
    last = len(partners)
    gqo[...] = gtx[last, 0] * factor
    gko[...] = gtx[last, 1] * factor

    for c in range(CHUNKS):
        for h in range(3):
            copy1(c, h, hops[h]).wait_send()
            copy2(c, h, hops[h]).wait_send()
        for s in range(len(dists)):
            for ab in range(2):
                @pl.when(sends(s, ab))
                def _():
                    copyz(c, s, ab).wait_send()
    for i in range(len(partners)):
        copyg(i).wait_send()


def solution(mesh):
    n = mesh.shape["seq"]
    ndp = mesh.shape["dp"]
    steps = max(1, (n // PLANE - 1).bit_length())
    gsteps = (n - 1).bit_length() + (ndp - 1).bit_length()

    def local(query_rows, key_rows, value_rows, out_grad, query_gain, key_gain):
        rows, width = query_rows.shape[1:]
        seq_len = rows * n
        score_scale = 1.0 / math.sqrt(HEAD_DIM * seq_len)
        factor = 1.0 / math.sqrt(seq_len * ndp)
        big = jax.ShapeDtypeStruct(query_rows.shape, BF16)
        small = jax.ShapeDtypeStruct((PAIRS, LANES), F32)
        vm = pl.BlockSpec(memory_space=pltpu.VMEM)
        hbm = pl.BlockSpec(memory_space=pltpu.HBM)
        unit = (2, HEAD_DIM, LANES)
        dma = pltpu.SemaphoreType.DMA
        out = pl.pallas_call(
            functools.partial(kernel, n, ndp, rows, score_scale, factor),
            out_shape=[big, big, big, small, small],
            in_specs=[hbm] * 4 + [vm] * 2,
            out_specs=[vm] * 5,
            scratch_shapes=[pltpu.VMEM((rows, width), BF16)] * 6
            + [pltpu.VMEM((rows, width), F32)] * 3
            + [
                pltpu.VMEM((CHUNKS, PLANE) + unit, F32),
                pltpu.VMEM((CHUNKS, PLANE) + unit, F32),
                pltpu.VMEM((steps, CHUNKS) + unit, F32),
                pltpu.VMEM((steps, CHUNKS) + unit, F32),
                pltpu.VMEM((CHUNKS,) + unit, F32),
                pltpu.VMEM((CHUNKS, PLANE) + unit, F32),
                pltpu.VMEM((CHUNKS, PLANE) + unit, F32),
                pltpu.VMEM((gsteps + 1, 2, PAIRS, LANES), F32),
                pltpu.VMEM((gsteps, 2, PAIRS, LANES), F32),
                dma((4,)),
                dma((CHUNKS, 3)), dma((CHUNKS, 3)),
                dma((steps, CHUNKS, 2)), dma((steps, CHUNKS, 2)),
                dma((CHUNKS, 3)), dma((CHUNKS, 3)),
                dma((gsteps,)), dma((gsteps,)),
            ],
            compiler_params=pltpu.CompilerParams(
                collective_id=0, has_side_effects=True, vmem_limit_bytes=32 * 1024 * 1024
            ),
        )(query_rows, key_rows, value_rows, out_grad,
          query_gain.reshape(PAIRS, LANES), key_gain.reshape(PAIRS, LANES))
        return (out[0], out[1], out[2], out[3].reshape(width), out[4].reshape(width))

    spec = P("dp", "seq", None)
    return jax.shard_map(local, mesh=mesh, in_specs=(spec,) * 4 + (P(), P()),
                         out_specs=(spec, spec, spec, P(), P()), check_vma=False)
```

time: 245 us -> 45.8 us (0.19)
  waiting for transfers between devices: 144 us -> 0 us
  blocking collectives: 52.7 us -> 0 us
  Pallas kernels: 0 us -> 36.4 us
  other arithmetic: 18.8 us -> 0 us
  between operations: 14.2 us -> 0.66 us
  matrix products: 4.32 us -> 0 us
    all_gather x2 -> x0, waiting for transfers between devices: 144 us -> none  [prefix(): gathered = lax.all_gather(part, axis)]
    psum x1 -> x0, blocking collectives: 52.7 us -> none  [local(): q_total, k_total = lax.psum((q_part, k_part), ('seq', 'dp'))]
    pallas_call x0 -> x1, Pallas kernels: none -> 36.4 us  [local(): pl.pallas_call(functools.partial(kernel, n, ndp, rows, score_scale, facto...]
    add x15 -> x0, other arithmetic: 15.1 us -> none  [add_one(): return earlier + later]
    unnamed x13 -> x17, local copies, waits for them, and re-layouts: 3.85 us -> 8.46 us
    dot_general x9 -> x0, matrix products: 4.32 us -> none  [the longest x1 1.75 us: local(): jnp.einsum('she,hde->shd', value_inputs, suffix_state, preferred_element_...]
  transfers between devices with their start and end apart: 2 -> 0, of which waited for: 2 -> 0; matrix products, arithmetic and copies ran while one was open for 3% -> 0% of each run, Pallas kernels for 0% -> 0%
where the time goes in v1:
time: 45.8 us; the launch traced here: 45.5 us
  Pallas kernels  36.4 us (79%)
  local copies, waits for them, and re-layouts  8.46 us (18%)
  between operations  0.66 us (1%)
    pallas_call x1, Pallas kernels, local(): pl.pallas_call(functools.partial(kernel, n, ndp, rows, score_scale, facto...  36.4 us
    unnamed x17, local copies, waits for them, and re-layouts  8.46 us

profile of v1, /device:TPU:0, one launch (start us, length us, event | category | flops | bytes accessed | tf_op | source)
XLA Modules:
  0.0 45.5 jit_solution(14103110488943375484)
XLA Ops:
  0.6 0.0 copy-start
  0.6 0.9 %copy-done = bf16[1,128,1024]{2,1,0:T(8,128)(2,1)S(1)} copy-done((bf16[1,128,1024]{2,1,0:T(8,128)(2,1)S(1)}, bf16[1,128,1024]{2,1,0:T(8,128)(2,1)}, u32[]{:S(2)}) %copy-start) | copy-done | bytes 262168
  1.6 0.0 copy-start.1
  1.6 0.9 %copy-done.1 = bf16[1,128,1024]{2,1,0:T(8,128)(2,1)S(1)} copy-done((bf16[1,128,1024]{2,1,0:T(8,128)(2,1)S(1)}, bf16[1,128,1024]{2,1,0:T(8,128)(2,1)}, u32[]{:S(2)}) %copy-start.1) | copy-done | bytes 262168
  2.5 0.0 copy-start.2
  2.5 0.9 %copy-done.2 = bf16[1,128,1024]{2,1,0:T(8,128)(2,1)S(1)} copy-done((bf16[1,128,1024]{2,1,0:T(8,128)(2,1)S(1)}, bf16[1,128,1024]{2,1,0:T(8,128)(2,1)}, u32[]{:S(2)}) %copy-start.2) | copy-done | bytes 262168
  3.5 0.0 copy-start.3
  3.5 0.9 %copy-done.3 = bf16[1,128,1024]{2,1,0:T(8,128)(2,1)S(1)} copy-done((bf16[1,128,1024]{2,1,0:T(8,128)(2,1)S(1)}, bf16[1,128,1024]{2,1,0:T(8,128)(2,1)}, u32[]{:S(2)}) %copy-start.3) | copy-done | bytes 262168
  4.4 0.0 copy-start.4
  4.4 0.7 %copy-done.4 = f32[1024]{0:T(1024)S(1)} copy-done((f32[1024]{0:T(1024)S(1)}, f32[1024]{0:T(1024)}, u32[]{:S(2)}) %copy-start.4) | copy-done | bytes 4120
  5.1 0.0 copy-start.5
  5.1 0.7 %copy-done.5 = f32[1024]{0:T(1024)S(1)} copy-done((f32[1024]{0:T(1024)S(1)}, f32[1024]{0:T(1024)}, u32[]{:S(2)}) %copy-start.5) | copy-done | bytes 4120
  5.8 36.4 %shard_map.101 = (bf16[1,128,1024]{2,1,0:T(8,128)(2,1)S(1)}, bf16[1,128,1024]{2,1,0:T(8,128)(2,1)S(1)}, bf16[1,128,1024]{2,1,0:T(8,128)(2,1)S(1)}, f32[8,128]{1,0:T(8,128)S(1)}, f32[8,128]{1,0:T(8,128)S(1)}) custom-call(bf16[1,128,1024]{2,1,0:T(8,128)(2,1)S(1)} %copy-done, bf16[1,128,1024]{2,1,0:T(8,128)(2,1)S(1)} %copy-done.1, ...), custom_call_target="tpu_custom_call" | custom-call | tf_op jit(solution)/shard_map/pallas_call | solution.py:273
  42.2 0.7 %copy.16 = bf16[1,128,1024]{2,1,0:T(8,128)(2,1)} copy(bf16[1,128,1024]{2,1,0:T(8,128)(2,1)S(1)} %get-tuple-element.20) | data formatting | bytes 524288
  42.9 0.7 %copy.17 = bf16[1,128,1024]{2,1,0:T(8,128)(2,1)} copy(bf16[1,128,1024]{2,1,0:T(8,128)(2,1)S(1)} %get-tuple-element.21) | data formatting | bytes 524288
  43.6 0.7 %copy.18 = bf16[1,128,1024]{2,1,0:T(8,128)(2,1)} copy(bf16[1,128,1024]{2,1,0:T(8,128)(2,1)S(1)} %get-tuple-element.22) | data formatting | bytes 524288
  44.3 0.6 %copy.19 = f32[1024]{0:T(1024)} copy(f32[1024]{0:T(1024)S(1)} %bitcast.7) | data formatting | bytes 8192
  44.9 0.6 %copy.20 = f32[1024]{0:T(1024)} copy(f32[1024]{0:T(1024)S(1)} %bitcast.6) | data formatting | bytes 8192
Async XLA Ops:
  0.6 1.0 %copy-start = (bf16[1,128,1024]{2,1,0:T(8,128)(2,1)S(1)}, bf16[1,128,1024]{2,1,0:T(8,128)(2,1)}, u32[]{:S(2)}) copy-start(bf16[1,128,1024]{2,1,0:T(8,128)(2,1)} %q_h.1) | copy-start | bytes 786436
  1.6 0.9 %copy-start.1 = (bf16[1,128,1024]{2,1,0:T(8,128)(2,1)S(1)}, bf16[1,128,1024]{2,1,0:T(8,128)(2,1)}, u32[]{:S(2)}) copy-start(bf16[1,128,1024]{2,1,0:T(8,128)(2,1)} %k_h.1) | copy-start | bytes 786436
  2.5 0.9 %copy-start.2 = (bf16[1,128,1024]{2,1,0:T(8,128)(2,1)S(1)}, bf16[1,128,1024]{2,1,0:T(8,128)(2,1)}, u32[]{:S(2)}) copy-start(bf16[1,128,1024]{2,1,0:T(8,128)(2,1)} %v_h.1) | copy-start | bytes 786436
  3.5 0.9 %copy-start.3 = (bf16[1,128,1024]{2,1,0:T(8,128)(2,1)S(1)}, bf16[1,128,1024]{2,1,0:T(8,128)(2,1)}, u32[]{:S(2)}) copy-start(bf16[1,128,1024]{2,1,0:T(8,128)(2,1)} %g_h.1) | copy-start | bytes 786436
  4.4 0.7 %copy-start.4 = (f32[1024]{0:T(1024)S(1)}, f32[1024]{0:T(1024)}, u32[]{:S(2)}) copy-start(f32[1024]{0:T(1024)} %param.10) | copy-start | bytes 12292
  5.1 0.7 %copy-start.5 = (f32[1024]{0:T(1024)S(1)}, f32[1024]{0:T(1024)}, u32[]{:S(2)}) copy-start(f32[1024]{0:T(1024)} %param.11) | copy-start | bytes 12292

commit v2 on v1

--- a/solution.py
+++ b/solution.py
@@ -17,17 +17,18 @@
 LANES = 2 * HEAD_DIM
 PAIRS = HEADS // 2
 CHUNKS = PAIRS // PLANE
+VMEM_BYTES = 60 * 1024 * 1024
 
 
 def dot(a, b, da, db):
     return lax.dot_general(a, b, (((da,), (db,)), ((), ())), preferred_element_type=F32)
 
 
-def kernel(n, ndp, rows, score_scale, factor, q_h, k_h, v_h, g_h, gain_q, gain_k,
+def kernel(n, ndp, rows, score_scale, factor, q_h, k_h, v_h, g_h, gq_h, gk_h,
            qo, ko, vo, gqo, gko,
-           qx, kx, vx, gx, gq, gk, dqs, dks, dvs,
+           qx, kx, vx, gx, gq, gk, qb, kb, vb, gain_q, gain_k, gqb, gkb, dqs, dks, dvs,
            own, rx1, zs, zr, exc, tx2, rx2, gtx, grx,
-           in_sem, s1, r1, sz, rz, s2, r2, sg, rg):
+           in_sem, gain_sem, out_sem, gout_sem, s1, r1, sz, rz, s2, r2, sg, rg):
     nz = n // PLANE
     dists = []
     d = 1
@@ -44,11 +45,21 @@
     fy = 2 - 4 * y
     hops = [fx, fy, fx + fy]
 
-    loads = []
-    for i, (src, dst) in enumerate(((k_h, kx), (v_h, vx), (q_h, qx), (g_h, gx))):
-        cp = pltpu.make_async_copy(src.at[0], dst, in_sem.at[i])
-        cp.start()
-        loads.append(cp)
+    span = PLANE * LANES
+
+    def part(c):
+        return pl.ds(c * span, span)
+
+    gains = []
+    for i, (src, dst) in enumerate(((gk_h, gain_k), (gq_h, gain_q))):
+        gains.append(pltpu.make_async_copy(src, dst, gain_sem.at[i]))
+        gains[i].start()
+    loads = {}
+    for c in range(CHUNKS):
+        for i, (src, dst) in enumerate(((k_h, kx), (v_h, vx), (q_h, qx), (g_h, gx))):
+            loads[c, i] = pltpu.make_async_copy(
+                src.at[0, :, part(c)], dst.at[:, part(c)], in_sem.at[c, i])
+            loads[c, i].start()
 
     barrier = pltpu.get_barrier_semaphore()
 
@@ -113,22 +124,25 @@
         return z >= dists[s] if ab == 0 else z + dists[s] < nz
 
     def own_states(c):
+        if c == 0:
+            gains[0].wait()
+        loads[c, 0].wait()
+        loads[c, 1].wait()
         for p in range(PLANE):
-            pair = p * CHUNKS + c
+            pair = c * PLANE + p
             gkp = (kx[:, cols(pair)].astype(F32) * gain_k[pair:pair + 1, :]).astype(BF16)
             gk[:, cols(pair)] = gkp
             own[c, p, 0] = fold(dot(gkp, vx[:, cols(pair)], 0, 0))
         if c == 0:
-            loads[2].wait()
-            loads[3].wait()
+            gains[1].wait()
+        loads[c, 2].wait()
+        loads[c, 3].wait()
         for p in range(PLANE):
-            pair = p * CHUNKS + c
+            pair = c * PLANE + p
             gqp = (qx[:, cols(pair)].astype(F32) * gain_q[pair:pair + 1, :]).astype(BF16)
             gq[:, cols(pair)] = gqp
             own[c, p, 1] = fold(dot(gqp, gx[:, cols(pair)], 0, 0))
 
-    loads[0].wait()
-    loads[1].wait()
     for c in range(CHUNKS):
         own_states(c)
         if c == 0:
@@ -150,16 +164,19 @@
         gv, vv, qv, kv = gx[:, sl], vx[:, sl], gq[:, sl], gk[:, sl]
         gs, qs = stack(gv), stack(qv)
         pg = jnp.where(low, dot(gv, stack(vv), 1, 1), 0.0).astype(BF16)
-        dqs[:, sl] = dot(pg, stack(kv), 1, 0)
+        dq = score_scale * dot(pg, stack(kv), 1, 0)
+        dqs[:, sl] = dq
+        gtx[0, 0, pair:pair + 1, :] = jnp.sum(dq * qx[:, sl].astype(F32), axis=0, keepdims=True)
         pgt = jnp.where(high, dot(vv, gs, 1, 1), 0.0).astype(BF16)
-        dks[:, sl] = dot(pgt, qs, 1, 0)
+        dk = score_scale * dot(pgt, qs, 1, 0)
+        dks[:, sl] = dk
+        gtx[0, 1, pair:pair + 1, :] = jnp.sum(dk * kx[:, sl].astype(F32), axis=0, keepdims=True)
         pst = jnp.where(high, dot(kv, qs, 1, 1), 0.0).astype(BF16)
-        dvs[:, sl] = dot(pst, gs, 1, 0)
-
-    for pair in range(PAIRS):
-        intra(pair)
-
-    for c in range(CHUNKS):
+        dvs[:, sl] = score_scale * dot(pst, gs, 1, 0)
+
+    steps = len(dists)
+
+    def totals(c):
         for h in range(3):
             copy1(c, h, hops[h]).wait_recv()
         zs[0, c] = (rx1[c, 0] + rx1[c, 1]) + (rx1[c, 2] + rx1[c, 3])
@@ -170,29 +187,30 @@
                 def _():
                     copyz(c, 0, ab).start()
 
-    for s in range(len(dists)):
-        for c in range(CHUNKS):
-            for ab in range(2):
-                @pl.when(takes(s, ab))
+    def scan(s, c):
+        for ab in range(2):
+            @pl.when(takes(s, ab))
+            def _():
+                copyz(c, s, ab).wait_recv()
+                got = zr[s, c, ab]
+                exc[c, ab] = exc[c, ab] + got
+                if s + 1 < steps:
+                    zs[s + 1, c, ab] = zs[s, c, ab] + got
+            if s + 1 < steps:
+                @pl.when(jnp.logical_not(takes(s, ab)))
                 def _():
-                    copyz(c, s, ab).wait_recv()
-                    got = zr[s, c, ab]
-                    exc[c, ab] = exc[c, ab] + got
-                    if s + 1 < len(dists):
-                        zs[s + 1, c, ab] = zs[s, c, ab] + got
-                if s + 1 < len(dists):
-                    @pl.when(jnp.logical_not(takes(s, ab)))
-                    def _():
-                        zs[s + 1, c, ab] = zs[s, c, ab]
-
-                    @pl.when(sends(s + 1, ab))
-                    def _():
-                        copyz(c, s + 1, ab).start()
-
-    for c in range(CHUNKS):
+                    zs[s + 1, c, ab] = zs[s, c, ab]
+
+                @pl.when(sends(s + 1, ab))
+                def _():
+                    copyz(c, s + 1, ab).start()
+
+    def give(c):
         run = exc[c, 0]
+        both = jnp.zeros_like(run)
         for p in range(PLANE):
             tx2[c, p, 0] = run
+            both = both + run * rx1[c, p, 1]
             if p + 1 < PLANE:
                 run = run + rx1[c, p, 0]
         run = exc[c, 1]
@@ -203,42 +221,80 @@
         for h in (2, 0, 1):
             copy2(c, h, hops[h]).start()
         rx2[c, slot] = tx2[c, slot]
-
-    for c in range(CHUNKS):
+        spread = jnp.concatenate([jnp.where(left, both, 0.0), jnp.where(left, 0.0, both)], axis=0)
+        line = lax.dot_general(
+            jnp.ones((8, LANES), F32), spread, (((1,), (1,)), ((), ())),
+            precision=lax.Precision.HIGHEST, preferred_element_type=F32)
+        gtx[0, 2, pl.ds(c * PLANE + slot, 1), :] = line[:1] * score_scale
+
+    def final(c):
         for h in range(3):
             copy2(c, h, hops[h]).wait_recv()
         for p in range(PLANE):
-            pair = p * CHUNKS + c
+            pair = c * PLANE + p
             sl = cols(pair)
             sa = stack(rx2[c, p, 0].astype(BF16))
             sb = stack(rx2[c, p, 1].astype(BF16))
-            dq = score_scale * (dqs[:, sl] + dot(gx[:, sl], sa, 1, 1))
-            dk = score_scale * (dks[:, sl] + dot(vx[:, sl], sb, 1, 1))
-            dv = score_scale * (dvs[:, sl] + dot(gk[:, sl], sb, 1, 0))
-            qo[0, :, sl] = (dq * gain_q[pair:pair + 1, :]).astype(BF16)
-            ko[0, :, sl] = (dk * gain_k[pair:pair + 1, :]).astype(BF16)
-            vo[0, :, sl] = dv.astype(BF16)
-            gtx[0, 0, pair:pair + 1, :] = jnp.sum(dq * qx[:, sl].astype(F32), axis=0, keepdims=True)
-            gtx[0, 1, pair:pair + 1, :] = jnp.sum(dk * kx[:, sl].astype(F32), axis=0, keepdims=True)
+            dq = dqs[:, sl] + score_scale * dot(gx[:, sl], sa, 1, 1)
+            dk = dks[:, sl] + score_scale * dot(vx[:, sl], sb, 1, 1)
+            dv = dvs[:, sl] + score_scale * dot(gk[:, sl], sb, 1, 0)
+            qb[:, sl] = (dq * gain_q[pair:pair + 1, :]).astype(BF16)
+            kb[:, sl] = (dk * gain_k[pair:pair + 1, :]).astype(BF16)
+            vb[:, sl] = dv.astype(BF16)
+        for i in range(3):
+            stores(c, i).start()
+
+    def stores(c, i):
+        src, dst = ((qb, qo), (kb, ko), (vb, vo))[i]
+        return pltpu.make_async_copy(src.at[:, part(c)], dst.at[0, :, part(c)], out_sem.at[c, i])
+
+    gtx[0, 2] = jnp.zeros((PAIRS, LANES), F32)
+    todo = list(range(PAIRS))
+
+    def fill(count):
+        for _ in range(min(count, len(todo))):
+            intra(todo.pop(0))
+
+    for c in range(CHUNKS):
+        fill(3)
+        totals(c)
+    for s in range(steps):
+        for c in range(CHUNKS):
+            if s == 0:
+                fill(1)
+            scan(s, c)
+            if s + 1 == steps:
+                fill(PAIRS)
+                give(c)
+    if not steps:
+        fill(PAIRS)
+        for c in range(CHUNKS):
+            give(c)
 
     partners = [{"dp": dp + d * (1 - 2 * ((dp // d) % 2))} for d in dp_bits]
-    d = 1
-    while d < n:
+    for d in [d * PLANE for d in dists] + [1, 2]:
         partners.append({"seq": me + d * (1 - 2 * ((me // d) % 2))})
-        d *= 2
 
     def copyg(i):
         return pltpu.make_async_remote_copy(
             src_ref=gtx.at[i], dst_ref=grx.at[i], send_sem=sg.at[i], recv_sem=rg.at[i],
             device_id=partners[i], device_id_type=MESH)
 
-    for i in range(len(partners)):
+    last = len(partners)
+    when = {last - 2 - (CHUNKS - 1 - c): c for c in range(CHUNKS - 1)}
+    for i in range(last):
         copyg(i).start()
+        if i in when:
+            final(when[i])
         copyg(i).wait_recv()
         gtx[i + 1] = gtx[i] + grx[i]
-    last = len(partners)
-    gqo[...] = gtx[last, 0] * factor
-    gko[...] = gtx[last, 1] * factor
+    gqb[...] = (gtx[last, 0] + gtx[last, 2] / gain_q[...]) * factor
+    gkb[...] = (gtx[last, 1] + gtx[last, 2] / gain_k[...]) * factor
+    gout = [pltpu.make_async_copy(gqb, gqo, gout_sem.at[0]),
+            pltpu.make_async_copy(gkb, gko, gout_sem.at[1])]
+    for cp in gout:
+        cp.start()
+    final(CHUNKS - 1)
 
     for c in range(CHUNKS):
         for h in range(3):
@@ -249,8 +305,23 @@
                 @pl.when(sends(s, ab))
                 def _():
                     copyz(c, s, ab).wait_send()
-    for i in range(len(partners)):
+    for i in range(last):
         copyg(i).wait_send()
+    for cp in gout:
+        cp.wait()
+    for c in range(CHUNKS):
+        for i in range(3):
+            stores(c, i).wait()
+
+
+def move(*refs):
+    sem = refs[-1]
+    half = (len(refs) - 1) // 2
+    copies = [pltpu.make_async_copy(refs[i], refs[half + i], sem.at[i]) for i in range(half)]
+    for cp in copies:
+        cp.start()
+    for cp in copies:
+        cp.wait()
 
 
 def solution(mesh):
@@ -266,16 +337,16 @@
         factor = 1.0 / math.sqrt(seq_len * ndp)
         big = jax.ShapeDtypeStruct(query_rows.shape, BF16)
         small = jax.ShapeDtypeStruct((PAIRS, LANES), F32)
-        vm = pl.BlockSpec(memory_space=pltpu.VMEM)
         hbm = pl.BlockSpec(memory_space=pltpu.HBM)
         unit = (2, HEAD_DIM, LANES)
         dma = pltpu.SemaphoreType.DMA
         out = pl.pallas_call(
             functools.partial(kernel, n, ndp, rows, score_scale, factor),
             out_shape=[big, big, big, small, small],
-            in_specs=[hbm] * 4 + [vm] * 2,
-            out_specs=[vm] * 5,
-            scratch_shapes=[pltpu.VMEM((rows, width), BF16)] * 6
+            in_specs=[hbm] * 6,
+            out_specs=[hbm] * 5,
+            scratch_shapes=[pltpu.VMEM((rows, width), BF16)] * 9
+            + [pltpu.VMEM((PAIRS, LANES), F32)] * 4
             + [pltpu.VMEM((rows, width), F32)] * 3
             + [
                 pltpu.VMEM((CHUNKS, PLANE) + unit, F32),
@@ -285,19 +356,27 @@
                 pltpu.VMEM((CHUNKS,) + unit, F32),
                 pltpu.VMEM((CHUNKS, PLANE) + unit, F32),
                 pltpu.VMEM((CHUNKS, PLANE) + unit, F32),
-                pltpu.VMEM((gsteps + 1, 2, PAIRS, LANES), F32),
-                pltpu.VMEM((gsteps, 2, PAIRS, LANES), F32),
-                dma((4,)),
+                pltpu.VMEM((gsteps + 1, 3, PAIRS, LANES), F32),
+                pltpu.VMEM((gsteps, 3, PAIRS, LANES), F32),
+                dma((CHUNKS, 4)), dma((2,)), dma((CHUNKS, 3)), dma((2,)),
                 dma((CHUNKS, 3)), dma((CHUNKS, 3)),
                 dma((steps, CHUNKS, 2)), dma((steps, CHUNKS, 2)),
                 dma((CHUNKS, 3)), dma((CHUNKS, 3)),
                 dma((gsteps,)), dma((gsteps,)),
             ],
             compiler_params=pltpu.CompilerParams(
-                collective_id=0, has_side_effects=True, vmem_limit_bytes=32 * 1024 * 1024
+                collective_id=0, has_side_effects=True, vmem_limit_bytes=VMEM_BYTES
             ),
         )(query_rows, key_rows, value_rows, out_grad,
           query_gain.reshape(PAIRS, LANES), key_gain.reshape(PAIRS, LANES))
+        out = pl.pallas_call(
+            move,
+            out_shape=[big, big, big, small, small],
+            in_specs=[hbm] * 5,
+            out_specs=[hbm] * 5,
+            scratch_shapes=[dma((5,))],
+            compiler_params=pltpu.CompilerParams(vmem_limit_bytes=VMEM_BYTES),
+        )(*out)
         return (out[0], out[1], out[2], out[3].reshape(width), out[4].reshape(width))
 
     spec = P("dp", "seq", None)

time: 45.8 us -> 57.4 us (1.25)
  Pallas kernels: 36.4 us -> 56.6 us
  local copies, waits for them, and re-layouts: 8.46 us -> 0 us
    pallas_call x0 -> x1, Pallas kernels: none -> 25.2 us  [local(): pl.pallas_call(move, out_shape=[big, big, big, small, small], in_specs=[h...]
    unnamed x17 -> x0, local copies, waits for them, and re-layouts: 8.46 us -> none
    pallas_call x1, Pallas kernels: 36.4 us -> 31.4 us  [local(): pl.pallas_call(functools.partial(kernel, n, ndp, rows, score_scale, facto...]
where the time goes in v2:
time: 57.4 us; the launch traced here: 57.2 us
  Pallas kernels  56.6 us (99%)
  between operations  0.64 us (1%)
    pallas_call x1, Pallas kernels, local(): pl.pallas_call(functools.partial(kernel, n, ndp, rows, score_scale, facto...  31.4 us
    pallas_call x1, Pallas kernels, local(): pl.pallas_call(move, out_shape=[big, big, big, small, small], in_specs=[h...  25.2 us

profile of v2, /device:TPU:0, one launch (start us, length us, event | category | flops | bytes accessed | tf_op | source)
XLA Modules:
  0.0 57.2 jit_solution(5196280197162470905)
XLA Ops:
  0.6 31.4 %shard_map.101 = (bf16[1,128,1024]{2,1,0:T(8,128)(2,1)}, bf16[1,128,1024]{2,1,0:T(8,128)(2,1)}, bf16[1,128,1024]{2,1,0:T(8,128)(2,1)}, f32[8,128]{1,0:T(8,128)}, f32[8,128]{1,0:T(8,128)}) custom-call(bf16[1,128,1024]{2,1,0:T(8,128)(2,1)} %q_h.1, bf16[1,128,1024]{2,1,0:T(8,128)(2,1)} %k_h.1, bf16[1,128,1024]{2,1,0:T(8,128)(2,1)} %v_h.1, ...), custom_call_target="tpu_custom_call" | custom-call | tf_op jit(solution)/shard_map/pallas_call | solution.py:343
  32.0 25.2 %shard_map.102 = (bf16[1,128,1024]{2,1,0:T(8,128)(2,1)}, bf16[1,128,1024]{2,1,0:T(8,128)(2,1)}, bf16[1,128,1024]{2,1,0:T(8,128)(2,1)}, f32[8,128]{1,0:T(8,128)}, f32[8,128]{1,0:T(8,128)}) custom-call(bf16[1,128,1024]{2,1,0:T(8,128)(2,1)} %get-tuple-element.15.refs_0_, bf16[1,128,1024]{2,1,0:T(8,128)(2,1)} %get-tuple-element.16.refs_1_, ...), custom_call_target="tpu_custom_call" | custom-call | tf_op jit(solution)/shard_map/pallas_call | solution.py:372

commit v3 on v2

--- a/solution.py
+++ b/solution.py
@@ -17,7 +17,6 @@
 LANES = 2 * HEAD_DIM
 PAIRS = HEADS // 2
 CHUNKS = PAIRS // PLANE
-VMEM_BYTES = 60 * 1024 * 1024
 
 
 def dot(a, b, da, db):
@@ -26,9 +25,9 @@
 
 def kernel(n, ndp, rows, score_scale, factor, q_h, k_h, v_h, g_h, gq_h, gk_h,
            qo, ko, vo, gqo, gko,
-           qx, kx, vx, gx, gq, gk, qb, kb, vb, gain_q, gain_k, gqb, gkb, dqs, dks, dvs,
+           qx, kx, vx, gx, gq, gk, gain_q, gain_k, dqs, dks, dvs,
            own, rx1, zs, zr, exc, tx2, rx2, gtx, grx,
-           in_sem, gain_sem, out_sem, gout_sem, s1, r1, sz, rz, s2, r2, sg, rg):
+           in_sem, gain_sem, s1, r1, sz, rz, s2, r2, sg, rg):
     nz = n // PLANE
     dists = []
     d = 1
@@ -238,15 +237,9 @@
             dq = dqs[:, sl] + score_scale * dot(gx[:, sl], sa, 1, 1)
             dk = dks[:, sl] + score_scale * dot(vx[:, sl], sb, 1, 1)
             dv = dvs[:, sl] + score_scale * dot(gk[:, sl], sb, 1, 0)
-            qb[:, sl] = (dq * gain_q[pair:pair + 1, :]).astype(BF16)
-            kb[:, sl] = (dk * gain_k[pair:pair + 1, :]).astype(BF16)
-            vb[:, sl] = dv.astype(BF16)
-        for i in range(3):
-            stores(c, i).start()
-
-    def stores(c, i):
-        src, dst = ((qb, qo), (kb, ko), (vb, vo))[i]
-        return pltpu.make_async_copy(src.at[:, part(c)], dst.at[0, :, part(c)], out_sem.at[c, i])
+            qo[0, :, sl] = (dq * gain_q[pair:pair + 1, :]).astype(BF16)
+            ko[0, :, sl] = (dk * gain_k[pair:pair + 1, :]).astype(BF16)
+            vo[0, :, sl] = dv.astype(BF16)
 
     gtx[0, 2] = jnp.zeros((PAIRS, LANES), F32)
     todo = list(range(PAIRS))
@@ -288,12 +281,8 @@
             final(when[i])
         copyg(i).wait_recv()
         gtx[i + 1] = gtx[i] + grx[i]
-    gqb[...] = (gtx[last, 0] + gtx[last, 2] / gain_q[...]) * factor
-    gkb[...] = (gtx[last, 1] + gtx[last, 2] / gain_k[...]) * factor
-    gout = [pltpu.make_async_copy(gqb, gqo, gout_sem.at[0]),
-            pltpu.make_async_copy(gkb, gko, gout_sem.at[1])]
-    for cp in gout:
-        cp.start()
+    gqo[...] = (gtx[last, 0] + gtx[last, 2] / gain_q[...]) * factor
+    gko[...] = (gtx[last, 1] + gtx[last, 2] / gain_k[...]) * factor
     final(CHUNKS - 1)
 
     for c in range(CHUNKS):
@@ -307,11 +296,6 @@
                     copyz(c, s, ab).wait_send()
     for i in range(last):
         copyg(i).wait_send()
-    for cp in gout:
-        cp.wait()
-    for c in range(CHUNKS):
-        for i in range(3):
-            stores(c, i).wait()
 
 
 def move(*refs):
@@ -344,9 +328,9 @@
             functools.partial(kernel, n, ndp, rows, score_scale, factor),
             out_shape=[big, big, big, small, small],
             in_specs=[hbm] * 6,
-            out_specs=[hbm] * 5,
-            scratch_shapes=[pltpu.VMEM((rows, width), BF16)] * 9
-            + [pltpu.VMEM((PAIRS, LANES), F32)] * 4
+            out_specs=[pl.BlockSpec(memory_space=pltpu.VMEM)] * 5,
+            scratch_shapes=[pltpu.VMEM((rows, width), BF16)] * 6
+            + [pltpu.VMEM((PAIRS, LANES), F32)] * 2
             + [pltpu.VMEM((rows, width), F32)] * 3
             + [
                 pltpu.VMEM((CHUNKS, PLANE) + unit, F32),
@@ -358,25 +342,25 @@
                 pltpu.VMEM((CHUNKS, PLANE) + unit, F32),
                 pltpu.VMEM((gsteps + 1, 3, PAIRS, LANES), F32),
                 pltpu.VMEM((gsteps, 3, PAIRS, LANES), F32),
-                dma((CHUNKS, 4)), dma((2,)), dma((CHUNKS, 3)), dma((2,)),
+                dma((CHUNKS, 4)), dma((2,)),
                 dma((CHUNKS, 3)), dma((CHUNKS, 3)),
                 dma((steps, CHUNKS, 2)), dma((steps, CHUNKS, 2)),
                 dma((CHUNKS, 3)), dma((CHUNKS, 3)),
                 dma((gsteps,)), dma((gsteps,)),
             ],
             compiler_params=pltpu.CompilerParams(
-                collective_id=0, has_side_effects=True, vmem_limit_bytes=VMEM_BYTES
+                collective_id=0, has_side_effects=True, vmem_limit_bytes=32 * 1024 * 1024
             ),
-        )(query_rows, key_rows, value_rows, out_grad,
-          query_gain.reshape(PAIRS, LANES), key_gain.reshape(PAIRS, LANES))
+        )(*[pltpu.with_memory_space_constraint(t, pltpu.HBM) for t in (
+            query_rows, key_rows, value_rows, out_grad,
+            query_gain.reshape(PAIRS, LANES), key_gain.reshape(PAIRS, LANES))])
         out = pl.pallas_call(
             move,
             out_shape=[big, big, big, small, small],
-            in_specs=[hbm] * 5,
+            in_specs=[pl.BlockSpec(memory_space=pltpu.VMEM)] * 5,
             out_specs=[hbm] * 5,
             scratch_shapes=[dma((5,))],
-            compiler_params=pltpu.CompilerParams(vmem_limit_bytes=VMEM_BYTES),
-        )(*out)
+        )(*[pltpu.with_memory_space_constraint(t, pltpu.VMEM) for t in out])
         return (out[0], out[1], out[2], out[3].reshape(width), out[4].reshape(width))
 
     spec = P("dp", "seq", None)

time: 57.4 us -> 32.3 us (0.56)
  Pallas kernels: 56.6 us -> 31.5 us
    pallas_call x1, Pallas kernels: 25.2 us -> 0.93 us  [local(): pl.pallas_call(move, out_shape=[big, big, big, small, small], in_specs=[p...]
    pallas_call x1, Pallas kernels: 31.4 us -> 30.6 us  [local(): pl.pallas_call(functools.partial(kernel, n, ndp, rows, score_scale, facto...]
where the time goes in v3:
time: 32.3 us; the launch traced here: 32.1 us
  Pallas kernels  31.5 us (98%)
  between operations  0.64 us (2%)
    pallas_call x1, Pallas kernels, local(): pl.pallas_call(functools.partial(kernel, n, ndp, rows, score_scale, facto...  30.6 us
    pallas_call x1, Pallas kernels, local(): pl.pallas_call(move, out_shape=[big, big, big, small, small], in_specs=[p...  0.93 us

profile of v3, /device:TPU:0, one launch (start us, length us, event | category | flops | bytes accessed | tf_op | source)
XLA Modules:
  0.0 32.1 jit_solution(6455905387862368026)
XLA Ops:
  0.6 30.6 %shard_map.101 = (bf16[1,128,1024]{2,1,0:T(8,128)(2,1)S(1)}, bf16[1,128,1024]{2,1,0:T(8,128)(2,1)S(1)}, bf16[1,128,1024]{2,1,0:T(8,128)(2,1)S(1)}, f32[8,128]{1,0:T(8,128)S(1)}, f32[8,128]{1,0:T(8,128)S(1)}) custom-call(bf16[1,128,1024]{2,1,0:T(8,128)(2,1)} %q_h.1, bf16[1,128,1024]{2,1,0:T(8,128)(2,1)} %k_h.1, bf16[1,128,1024]{2,1,0:T(8,128)(2,1)} %v_h.1, ...), custom_call_target="tpu_custom_call" | custom-call | tf_op jit(solution)/shard_map/pallas_call | solution.py:327
  31.2 0.9 %shard_map.102 = (bf16[1,128,1024]{2,1,0:T(8,128)(2,1)}, bf16[1,128,1024]{2,1,0:T(8,128)(2,1)}, bf16[1,128,1024]{2,1,0:T(8,128)(2,1)}, f32[8,128]{1,0:T(8,128)}, f32[8,128]{1,0:T(8,128)}) custom-call(bf16[1,128,1024]{2,1,0:T(8,128)(2,1)S(1)} %get-tuple-element.15.refs_0_, bf16[1,128,1024]{2,1,0:T(8,128)(2,1)S(1)} %get-tuple-element.16.refs_1_, ...), custom_call_target="tpu_custom_call" | custom-call | tf_op jit(solution)/shard_map/pallas_call | solution.py:357

commit v4 on v3

v4 whole, which is shorter than its diff:
```python
import functools
import math

import jax
import jax.numpy as jnp
from jax import lax
from jax.experimental import pallas as pl
from jax.experimental.pallas import tpu as pltpu
from jax.sharding import PartitionSpec as P

HEADS = 16
HEAD_DIM = 64
PLANE = 4
MESH = pl.DeviceIdType.MESH
F32 = jnp.float32
BF16 = jnp.bfloat16
LANES = 2 * HEAD_DIM
PAIRS = HEADS // 2
CHUNKS = PAIRS // PLANE


def dot(a, b, da, db):
    return lax.dot_general(a, b, (((da,), (db,)), ((), ())), preferred_element_type=F32)


def kernel(n, ndp, rows, score_scale, factor, q_h, k_h, v_h, g_h, gq_h, gk_h,
           qo, ko, vo, gqo, gko,
           qx, kx, vx, gx, gq, gk, gain_q, gain_k, dqs, dks, dvs,
           own, rx1, zs, zr, exc, tx2, rx2, gtx, grx, gpl,
           in_sem, gain_sem, s1, r1, sz, rz, s2, r2, sg, rg, sp, rp):
    nz = n // PLANE
    dists = []
    d = 1
    while d < nz:
        dists.append(d)
        d *= 2
    me = lax.axis_index("seq")
    dp = lax.axis_index("dp")
    z = me // PLANE
    slot = me % PLANE
    x = slot % 2
    y = slot // 2
    fx = 1 - 2 * x
    fy = 2 - 4 * y
    hops = [fx, fy, fx + fy]

    barrier = pltpu.get_barrier_semaphore()

    def greet(**where):
        pl.semaphore_signal(barrier, inc=1, device_id=where, device_id_type=MESH)

    for h in hops:
        greet(seq=me + h)
    for d in dists:
        @pl.when(z + d < nz)
        def _(d=d):
            greet(seq=me + d * PLANE)

        @pl.when(z >= d)
        def _(d=d):
            greet(seq=me - d * PLANE)
    dp_bits = []
    d = 1
    while d < ndp:
        dp_bits.append(d)
        d *= 2
    for d in dp_bits:
        greet(dp=dp + d * (1 - 2 * ((dp // d) % 2)))

    span = PLANE * LANES

    def part(c):
        return pl.ds(c * span, span)

    gains = []
    for i, (src, dst) in enumerate(((gk_h, gain_k), (gq_h, gain_q))):
        gains.append(pltpu.make_async_copy(src, dst, gain_sem.at[i]))
        gains[i].start()
    loads = {}
    for c in range(CHUNKS):
        for i, (src, dst) in enumerate(((k_h, kx), (v_h, vx), (q_h, qx), (g_h, gx))):
            loads[c, i] = pltpu.make_async_copy(
                src.at[0, :, part(c)], dst.at[:, part(c)], in_sem.at[c, i])
            loads[c, i].start()

    lane = lax.broadcasted_iota(jnp.int32, (1, LANES), 1)
    first = (lane < HEAD_DIM).astype(F32).astype(BF16)
    second = (lane >= HEAD_DIM).astype(F32).astype(BF16)
    left = lax.broadcasted_iota(jnp.int32, (HEAD_DIM, LANES), 1) < HEAD_DIM

    def stack(t):
        return jnp.concatenate([t * first, t * second], axis=0)

    def cols(pair):
        return pl.ds(pair * LANES, LANES)

    def fold(full):
        return jnp.where(left, full[:HEAD_DIM], full[HEAD_DIM:])

    def copy1(c, ab, h):
        hop = hops[h]
        return pltpu.make_async_remote_copy(
            src_ref=own.at[c, ab, slot + hop], dst_ref=rx1.at[c, ab, slot],
            send_sem=s1.at[c, ab, h], recv_sem=r1.at[c, ab, h],
            device_id={"seq": me + hop}, device_id_type=MESH)

    def copy2(c, ab, h):
        hop = hops[h]
        return pltpu.make_async_remote_copy(
            src_ref=tx2.at[c, ab, slot + hop], dst_ref=rx2.at[c, ab, slot],
            send_sem=s2.at[c, ab, h], recv_sem=r2.at[c, ab, h],
            device_id={"seq": me + hop}, device_id_type=MESH)

    def copyz(c, s, ab):
        to = me + dists[s] * PLANE if ab == 0 else me - dists[s] * PLANE
        return pltpu.make_async_remote_copy(
            src_ref=zs.at[s, c, ab], dst_ref=zr.at[s, c, ab],
            send_sem=sz.at[s, c, ab], recv_sem=rz.at[s, c, ab],
            device_id={"seq": to}, device_id_type=MESH)

    def sends(s, ab):
        return z + dists[s] < nz if ab == 0 else z >= dists[s]

    def takes(s, ab):
        return z >= dists[s] if ab == 0 else z + dists[s] < nz

    def own_state(c, ab):
        raw, gain, mult, other = ((kx, gain_k, gk, vx), (qx, gain_q, gq, gx))[ab]
        if c == 0:
            gains[ab].wait()
        loads[c, 2 * ab].wait()
        loads[c, 2 * ab + 1].wait()
        for p in range(PLANE):
            pair = c * PLANE + p
            t = (raw[:, cols(pair)].astype(F32) * gain[pair:pair + 1, :]).astype(BF16)
            mult[:, cols(pair)] = t
            own[c, ab, p] = fold(dot(t, other[:, cols(pair)], 0, 0))

    units = [(c, ab) for c in range(CHUNKS) for ab in range(2)]
    for c, ab in units:
        own_state(c, ab)
        if (c, ab) == (0, 0):
            count = len(hops) + len(dp_bits)
            for d in dists:
                count = count + (z + d < nz).astype(jnp.int32) + (z >= d).astype(jnp.int32)
            pl.semaphore_wait(barrier, count)
        for h in (2, 0, 1):
            copy1(c, ab, h).start()
        rx1[c, ab, slot] = own[c, ab, slot]

    row = lax.broadcasted_iota(jnp.int32, (rows, 2 * rows), 0)
    col = lax.broadcasted_iota(jnp.int32, (rows, 2 * rows), 1) % rows
    low = row >= col
    high = col >= row

    def intra(pair):
        sl = cols(pair)
        gv, vv, qv, kv = gx[:, sl], vx[:, sl], gq[:, sl], gk[:, sl]
        gs, qs = stack(gv), stack(qv)
        pg = jnp.where(low, dot(gv, stack(vv), 1, 1), 0.0).astype(BF16)
        dq = score_scale * dot(pg, stack(kv), 1, 0)
        dqs[:, sl] = dq
        gtx[0, 0, pair:pair + 1, :] = jnp.sum(dq * qx[:, sl].astype(F32), axis=0, keepdims=True)
        pgt = jnp.where(high, dot(vv, gs, 1, 1), 0.0).astype(BF16)
        dk = score_scale * dot(pgt, qs, 1, 0)
        dks[:, sl] = dk
        gtx[0, 1, pair:pair + 1, :] = jnp.sum(dk * kx[:, sl].astype(F32), axis=0, keepdims=True)
        pst = jnp.where(high, dot(kv, qs, 1, 1), 0.0).astype(BF16)
        dvs[:, sl] = score_scale * dot(pst, gs, 1, 0)

    steps = len(dists)

    def totals(c, ab):
        for h in range(3):
            copy1(c, ab, h).wait_recv()
        zs[0, c, ab] = (rx1[c, ab, 0] + rx1[c, ab, 1]) + (rx1[c, ab, 2] + rx1[c, ab, 3])
        exc[c, ab] = jnp.zeros_like(exc[c, ab])
        if dists:
            @pl.when(sends(0, ab))
            def _():
                copyz(c, 0, ab).start()

    def scan(s, c, ab):
        @pl.when(takes(s, ab))
        def _():
            copyz(c, s, ab).wait_recv()
            got = zr[s, c, ab]
            exc[c, ab] = exc[c, ab] + got
            if s + 1 < steps:
                zs[s + 1, c, ab] = zs[s, c, ab] + got
        if s + 1 < steps:
            @pl.when(jnp.logical_not(takes(s, ab)))
            def _():
                zs[s + 1, c, ab] = zs[s, c, ab]

            @pl.when(sends(s + 1, ab))
            def _():
                copyz(c, s + 1, ab).start()

    def give(c, ab):
        run = exc[c, ab]
        order = list(range(PLANE)) if ab == 0 else list(reversed(range(PLANE)))
        for p in order:
            tx2[c, ab, p] = run
            if p != order[-1]:
                run = run + rx1[c, ab, p]
        for h in (2, 0, 1):
            copy2(c, ab, h).start()
        rx2[c, ab, slot] = tx2[c, ab, slot]
        if ab == 0:
            return
        both = tx2[c, 0, 0] * rx1[c, 1, 0]
        for p in range(1, PLANE):
            both = both + tx2[c, 0, p] * rx1[c, 1, p]
        spread = jnp.concatenate([jnp.where(left, both, 0.0), jnp.where(left, 0.0, both)], axis=0)
        line = lax.dot_general(
            jnp.ones((8, LANES), F32), spread, (((1,), (1,)), ((), ())),
            precision=lax.Precision.HIGHEST, preferred_element_type=F32)
        gtx[0, 2, pl.ds(c * PLANE + slot, 1), :] = line[:1] * score_scale

    def final(c):
        for ab in range(2):
            for h in range(3):
                copy2(c, ab, h).wait_recv()
        for p in range(PLANE):
            pair = c * PLANE + p
            sl = cols(pair)
            sa = stack(rx2[c, 0, p].astype(BF16))
            sb = stack(rx2[c, 1, p].astype(BF16))
            dq = dqs[:, sl] + score_scale * dot(gx[:, sl], sa, 1, 1)
            dk = dks[:, sl] + score_scale * dot(vx[:, sl], sb, 1, 1)
            dv = dvs[:, sl] + score_scale * dot(gk[:, sl], sb, 1, 0)
            qo[0, :, sl] = (dq * gain_q[pair:pair + 1, :]).astype(BF16)
            ko[0, :, sl] = (dk * gain_k[pair:pair + 1, :]).astype(BF16)
            vo[0, :, sl] = dv.astype(BF16)

    gtx[0, 2] = jnp.zeros((PAIRS, LANES), F32)
    for pair in range(PAIRS):
        intra(pair)
    for turn in range(len(units) + steps):
        for stage in range(steps + 1):
            if 0 <= turn - stage < len(units):
                c, ab = units[turn - stage]
                if stage == 0:
                    totals(c, ab)
                else:
                    scan(stage - 1, c, ab)
                if stage == steps:
                    give(c, ab)

    partners = [{"dp": dp + d * (1 - 2 * ((dp // d) % 2))} for d in dp_bits]
    for d in [d * PLANE for d in dists]:
        partners.append({"seq": me + d * (1 - 2 * ((me // d) % 2))})

    def copyg(i):
        return pltpu.make_async_remote_copy(
            src_ref=gtx.at[i], dst_ref=grx.at[i], send_sem=sg.at[i], recv_sem=rg.at[i],
            device_id=partners[i], device_id_type=MESH)

    def copyp(h):
        return pltpu.make_async_remote_copy(
            src_ref=gtx.at[last], dst_ref=gpl.at[slot], send_sem=sp.at[h], recv_sem=rp.at[h],
            device_id={"seq": me + hops[h]}, device_id_type=MESH)

    last = len(partners)
    for i in range(last):
        copyg(i).start()
        copyg(i).wait_recv()
        gtx[i + 1] = gtx[i] + grx[i]
    for h in (2, 0, 1):
        copyp(h).start()
    gpl[slot] = gtx[last]
    for c in range(CHUNKS):
        final(c)
    for h in range(3):
        copyp(h).wait_recv()
    total = (gpl[0] + gpl[1]) + (gpl[2] + gpl[3])
    gqo[...] = (total[0] + total[2] / gain_q[...]) * factor
    gko[...] = (total[1] + total[2] / gain_k[...]) * factor

    for c in range(CHUNKS):
        for ab in range(2):
            for h in range(3):
                copy1(c, ab, h).wait_send()
                copy2(c, ab, h).wait_send()
        for s in range(len(dists)):
            for ab in range(2):
                @pl.when(sends(s, ab))
                def _():
                    copyz(c, s, ab).wait_send()
    for i in range(last):
        copyg(i).wait_send()
    for h in range(3):
        copyp(h).wait_send()


def move(*refs):
    sem = refs[-1]
    half = (len(refs) - 1) // 2
    copies = [pltpu.make_async_copy(refs[i], refs[half + i], sem.at[i]) for i in range(half)]
    for cp in copies:
        cp.start()
    for cp in copies:
        cp.wait()


def solution(mesh):
    n = mesh.shape["seq"]
    ndp = mesh.shape["dp"]
    steps = max(1, (n // PLANE - 1).bit_length())
    gsteps = max(1, (n // PLANE - 1).bit_length() + (ndp - 1).bit_length())

    def local(query_rows, key_rows, value_rows, out_grad, query_gain, key_gain):
        rows, width = query_rows.shape[1:]
        seq_len = rows * n
        score_scale = 1.0 / math.sqrt(HEAD_DIM * seq_len)
        factor = 1.0 / math.sqrt(seq_len * ndp)
        big = jax.ShapeDtypeStruct(query_rows.shape, BF16)
        small = jax.ShapeDtypeStruct((PAIRS, LANES), F32)
        hbm = pl.BlockSpec(memory_space=pltpu.HBM)
        unit = (HEAD_DIM, LANES)
        dma = pltpu.SemaphoreType.DMA
        out = pl.pallas_call(
            functools.partial(kernel, n, ndp, rows, score_scale, factor),
            out_shape=[big, big, big, small, small],
            in_specs=[hbm] * 6,
            out_specs=[pl.BlockSpec(memory_space=pltpu.VMEM)] * 5,
            scratch_shapes=[pltpu.VMEM((rows, width), BF16)] * 6
            + [pltpu.VMEM((PAIRS, LANES), F32)] * 2
            + [pltpu.VMEM((rows, width), F32)] * 3
            + [
                pltpu.VMEM((CHUNKS, 2, PLANE) + unit, F32),
                pltpu.VMEM((CHUNKS, 2, PLANE) + unit, F32),
                pltpu.VMEM((steps, CHUNKS, 2) + unit, F32),
                pltpu.VMEM((steps, CHUNKS, 2) + unit, F32),
                pltpu.VMEM((CHUNKS, 2) + unit, F32),
                pltpu.VMEM((CHUNKS, 2, PLANE) + unit, F32),
                pltpu.VMEM((CHUNKS, 2, PLANE) + unit, F32),
                pltpu.VMEM((gsteps + 1, 3, PAIRS, LANES), F32),
                pltpu.VMEM((gsteps, 3, PAIRS, LANES), F32),
                pltpu.VMEM((PLANE, 3, PAIRS, LANES), F32),
                dma((CHUNKS, 4)), dma((2,)),
                dma((CHUNKS, 2, 3)), dma((CHUNKS, 2, 3)),
                dma((steps, CHUNKS, 2)), dma((steps, CHUNKS, 2)),
                dma((CHUNKS, 2, 3)), dma((CHUNKS, 2, 3)),
                dma((gsteps,)), dma((gsteps,)), dma((3,)), dma((3,)),
            ],
            compiler_params=pltpu.CompilerParams(
                collective_id=0, has_side_effects=True, vmem_limit_bytes=32 * 1024 * 1024
            ),
        )(*[pltpu.with_memory_space_constraint(t, pltpu.HBM) for t in (
            query_rows, key_rows, value_rows, out_grad,
            query_gain.reshape(PAIRS, LANES), key_gain.reshape(PAIRS, LANES))])
        out = pl.pallas_call(
            move,
            out_shape=[big, big, big, small, small],
            in_specs=[pl.BlockSpec(memory_space=pltpu.VMEM)] * 5,
            out_specs=[hbm] * 5,
            scratch_shapes=[dma((5,))],
        )(*[pltpu.with_memory_space_constraint(t, pltpu.VMEM) for t in out])
        return (out[0], out[1], out[2], out[3].reshape(width), out[4].reshape(width))

    spec = P("dp", "seq", None)
    return jax.shard_map(local, mesh=mesh, in_specs=(spec,) * 4 + (P(), P()),
                         out_specs=(spec, spec, spec, P(), P()), check_vma=False)
```

time: 32.3 us -> 30.5 us (0.944)
  the two profiles are of different devices: /device:TPU:0 before, /device:TPU:24 now
where the time goes in v4:
time: 30.5 us; the launch traced here: 30.3 us
  Pallas kernels  29.7 us (97%)
  between operations  0.64 us (2%)
    pallas_call x1, Pallas kernels, local(): pl.pallas_call(functools.partial(kernel, n, ndp, rows, score_scale, facto...  28.7 us
    pallas_call x1, Pallas kernels, local(): pl.pallas_call(move, out_shape=[big, big, big, small, small], in_specs=[p...  0.93 us

profile of v4, /device:TPU:24, one launch (start us, length us, event | category | flops | bytes accessed | tf_op | source)
XLA Modules:
  0.0 30.3 jit_solution(10901002086541783084)
XLA Ops:
  0.6 28.7 %shard_map.101 = (bf16[1,128,1024]{2,1,0:T(8,128)(2,1)S(1)}, bf16[1,128,1024]{2,1,0:T(8,128)(2,1)S(1)}, bf16[1,128,1024]{2,1,0:T(8,128)(2,1)S(1)}, f32[8,128]{1,0:T(8,128)S(1)}, f32[8,128]{1,0:T(8,128)S(1)}) custom-call(bf16[1,128,1024]{2,1,0:T(8,128)(2,1)} %q_h.1, bf16[1,128,1024]{2,1,0:T(8,128)(2,1)} %k_h.1, bf16[1,128,1024]{2,1,0:T(8,128)(2,1)} %v_h.1, ...), custom_call_target="tpu_custom_call" | custom-call | tf_op jit(solution)/shard_map/pallas_call | solution.py:323
  29.4 0.9 %shard_map.102 = (bf16[1,128,1024]{2,1,0:T(8,128)(2,1)}, bf16[1,128,1024]{2,1,0:T(8,128)(2,1)}, bf16[1,128,1024]{2,1,0:T(8,128)(2,1)}, f32[8,128]{1,0:T(8,128)}, f32[8,128]{1,0:T(8,128)}) custom-call(bf16[1,128,1024]{2,1,0:T(8,128)(2,1)S(1)} %get-tuple-element.15.refs_0_, bf16[1,128,1024]{2,1,0:T(8,128)(2,1)S(1)} %get-tuple-element.16.refs_1_, ...), custom_call_target="tpu_custom_call" | custom-call | tf_op jit(solution)/shard_map/pallas_call | solution.py:354

commit v5 on v4

--- a/solution.py
+++ b/solution.py
@@ -17,6 +17,8 @@
 LANES = 2 * HEAD_DIM
 PAIRS = HEADS // 2
 CHUNKS = PAIRS // PLANE
+AHEAD = 3
+HOLD = 2
 
 
 def dot(a, b, da, db):
@@ -29,11 +31,8 @@
            own, rx1, zs, zr, exc, tx2, rx2, gtx, grx, gpl,
            in_sem, gain_sem, s1, r1, sz, rz, s2, r2, sg, rg, sp, rp):
     nz = n // PLANE
-    dists = []
-    d = 1
-    while d < nz:
-        dists.append(d)
-        d *= 2
+    dists = list(range(1, nz))
+    z_bits = [d for d in dists if d & (d - 1) == 0]
     me = lax.axis_index("seq")
     dp = lax.axis_index("dp")
     z = me // PLANE
@@ -114,7 +113,7 @@
     def copyz(c, s, ab):
         to = me + dists[s] * PLANE if ab == 0 else me - dists[s] * PLANE
         return pltpu.make_async_remote_copy(
-            src_ref=zs.at[s, c, ab], dst_ref=zr.at[s, c, ab],
+            src_ref=zs.at[0, c, ab], dst_ref=zr.at[s, c, ab],
             send_sem=sz.at[s, c, ab], recv_sem=rz.at[s, c, ab],
             device_id={"seq": to}, device_id_type=MESH)
 
@@ -137,7 +136,8 @@
             own[c, ab, p] = fold(dot(t, other[:, cols(pair)], 0, 0))
 
     units = [(c, ab) for c in range(CHUNKS) for ab in range(2)]
-    for c, ab in units:
+
+    def send(c, ab):
         own_state(c, ab)
         if (c, ab) == (0, 0):
             count = len(hops) + len(dp_bits)
@@ -147,6 +147,9 @@
         for h in (2, 0, 1):
             copy1(c, ab, h).start()
         rx1[c, ab, slot] = own[c, ab, slot]
+
+    for u in units[:AHEAD]:
+        send(*u)
 
     row = lax.broadcasted_iota(jnp.int32, (rows, 2 * rows), 0)
     col = lax.broadcasted_iota(jnp.int32, (rows, 2 * rows), 1) % rows
@@ -168,34 +171,23 @@
         pst = jnp.where(high, dot(kv, qs, 1, 1), 0.0).astype(BF16)
         dvs[:, sl] = score_scale * dot(pst, gs, 1, 0)
 
-    steps = len(dists)
 
     def totals(c, ab):
         for h in range(3):
             copy1(c, ab, h).wait_recv()
         zs[0, c, ab] = (rx1[c, ab, 0] + rx1[c, ab, 1]) + (rx1[c, ab, 2] + rx1[c, ab, 3])
         exc[c, ab] = jnp.zeros_like(exc[c, ab])
-        if dists:
-            @pl.when(sends(0, ab))
+        for s in range(len(dists)):
+            @pl.when(sends(s, ab))
             def _():
-                copyz(c, 0, ab).start()
-
-    def scan(s, c, ab):
-        @pl.when(takes(s, ab))
-        def _():
-            copyz(c, s, ab).wait_recv()
-            got = zr[s, c, ab]
-            exc[c, ab] = exc[c, ab] + got
-            if s + 1 < steps:
-                zs[s + 1, c, ab] = zs[s, c, ab] + got
-        if s + 1 < steps:
-            @pl.when(jnp.logical_not(takes(s, ab)))
+                copyz(c, s, ab).start()
+
+    def scan(c, ab):
+        for s in range(len(dists)):
+            @pl.when(takes(s, ab))
             def _():
-                zs[s + 1, c, ab] = zs[s, c, ab]
-
-            @pl.when(sends(s + 1, ab))
-            def _():
-                copyz(c, s + 1, ab).start()
+                copyz(c, s, ab).wait_recv()
+                exc[c, ab] = exc[c, ab] + zr[s, c, ab]
 
     def give(c, ab):
         run = exc[c, ab]
@@ -204,19 +196,21 @@
             tx2[c, ab, p] = run
             if p != order[-1]:
                 run = run + rx1[c, ab, p]
+        if ab == 0:
+            both = tx2[c, 0, 0] * rx1[c, 1, 0]
+            for p in range(1, PLANE):
+                both = both + tx2[c, 0, p] * rx1[c, 1, p]
+            spread = jnp.concatenate(
+                [jnp.where(left, both, 0.0), jnp.where(left, 0.0, both)], axis=0)
+            line = lax.dot_general(
+                jnp.ones((8, LANES), F32), spread, (((1,), (1,)), ((), ())),
+                precision=lax.Precision.HIGHEST, preferred_element_type=F32)
+            gtx[0, 2, pl.ds(c * PLANE + slot, 1), :] = line[:1] * score_scale
+            if c == CHUNKS - 1 and last:
+                copyg(0).start()
         for h in (2, 0, 1):
             copy2(c, ab, h).start()
         rx2[c, ab, slot] = tx2[c, ab, slot]
-        if ab == 0:
-            return
-        both = tx2[c, 0, 0] * rx1[c, 1, 0]
-        for p in range(1, PLANE):
-            both = both + tx2[c, 0, p] * rx1[c, 1, p]
-        spread = jnp.concatenate([jnp.where(left, both, 0.0), jnp.where(left, 0.0, both)], axis=0)
-        line = lax.dot_general(
-            jnp.ones((8, LANES), F32), spread, (((1,), (1,)), ((), ())),
-            precision=lax.Precision.HIGHEST, preferred_element_type=F32)
-        gtx[0, 2, pl.ds(c * PLANE + slot, 1), :] = line[:1] * score_scale
 
     def final(c):
         for ab in range(2):
@@ -235,21 +229,8 @@
             vo[0, :, sl] = dv.astype(BF16)
 
     gtx[0, 2] = jnp.zeros((PAIRS, LANES), F32)
-    for pair in range(PAIRS):
-        intra(pair)
-    for turn in range(len(units) + steps):
-        for stage in range(steps + 1):
-            if 0 <= turn - stage < len(units):
-                c, ab = units[turn - stage]
-                if stage == 0:
-                    totals(c, ab)
-                else:
-                    scan(stage - 1, c, ab)
-                if stage == steps:
-                    give(c, ab)
-
     partners = [{"dp": dp + d * (1 - 2 * ((dp // d) % 2))} for d in dp_bits]
-    for d in [d * PLANE for d in dists]:
+    for d in [d * PLANE for d in z_bits]:
         partners.append({"seq": me + d * (1 - 2 * ((me // d) % 2))})
 
     def copyg(i):
@@ -263,8 +244,22 @@
             device_id={"seq": me + hops[h]}, device_id_type=MESH)
 
     last = len(partners)
+    left_over = list(range(PAIRS))
+    for turn in range(len(units) + HOLD):
+        if turn < len(units):
+            totals(*units[turn])
+            if turn + AHEAD < len(units):
+                send(*units[turn + AHEAD])
+            if turn + AHEAD + 1 >= len(units):
+                while left_over:
+                    intra(left_over.pop(0))
+        if turn >= HOLD:
+            scan(*units[turn - HOLD])
+            give(*units[turn - HOLD])
+
     for i in range(last):
-        copyg(i).start()
+        if i > 0:
+            copyg(i).start()
         copyg(i).wait_recv()
         gtx[i + 1] = gtx[i] + grx[i]
     for h in (2, 0, 1):
@@ -307,7 +302,7 @@
 def solution(mesh):
     n = mesh.shape["seq"]
     ndp = mesh.shape["dp"]
-    steps = max(1, (n // PLANE - 1).bit_length())
+    steps = max(1, n // PLANE - 1)
     gsteps = max(1, (n // PLANE - 1).bit_length() + (ndp - 1).bit_length())
 
     def local(query_rows, key_rows, value_rows, out_grad, query_gain, key_gain):
@@ -331,7 +326,7 @@
             + [
                 pltpu.VMEM((CHUNKS, 2, PLANE) + unit, F32),
                 pltpu.VMEM((CHUNKS, 2, PLANE) + unit, F32),
-                pltpu.VMEM((steps, CHUNKS, 2) + unit, F32),
+                pltpu.VMEM((1, CHUNKS, 2) + unit, F32),
                 pltpu.VMEM((steps, CHUNKS, 2) + unit, F32),
                 pltpu.VMEM((CHUNKS, 2) + unit, F32),
                 pltpu.VMEM((CHUNKS, 2, PLANE) + unit, F32),

time: 30.5 us -> 28.7 us (0.941)
  the two profiles are of different devices: /device:TPU:24 before, /device:TPU:0 now
where the time goes in v5:
time: 28.7 us; the launch traced here: 28.5 us
  Pallas kernels  27.9 us (97%)
  between operations  0.64 us (2%)
    pallas_call x1, Pallas kernels, local(): pl.pallas_call(functools.partial(kernel, n, ndp, rows, score_scale, facto...  27 us
    pallas_call x1, Pallas kernels, local(): pl.pallas_call(move, out_shape=[big, big, big, small, small], in_specs=[p...  0.93 us

profile of v5, /device:TPU:0, one launch (start us, length us, event | category | flops | bytes accessed | tf_op | source)
XLA Modules:
  0.0 28.5 jit_solution(1191753831575428840)
XLA Ops:
  0.6 27.0 %shard_map.101 = (bf16[1,128,1024]{2,1,0:T(8,128)(2,1)S(1)}, bf16[1,128,1024]{2,1,0:T(8,128)(2,1)S(1)}, bf16[1,128,1024]{2,1,0:T(8,128)(2,1)S(1)}, f32[8,128]{1,0:T(8,128)S(1)}, f32[8,128]{1,0:T(8,128)S(1)}) custom-call(bf16[1,128,1024]{2,1,0:T(8,128)(2,1)} %q_h.1, bf16[1,128,1024]{2,1,0:T(8,128)(2,1)} %k_h.1, bf16[1,128,1024]{2,1,0:T(8,128)(2,1)} %v_h.1, ...), custom_call_target="tpu_custom_call" | custom-call | tf_op jit(solution)/shard_map/pallas_call | solution.py:318
  27.6 0.9 %shard_map.102 = (bf16[1,128,1024]{2,1,0:T(8,128)(2,1)}, bf16[1,128,1024]{2,1,0:T(8,128)(2,1)}, bf16[1,128,1024]{2,1,0:T(8,128)(2,1)}, f32[8,128]{1,0:T(8,128)}, f32[8,128]{1,0:T(8,128)}) custom-call(bf16[1,128,1024]{2,1,0:T(8,128)(2,1)S(1)} %get-tuple-element.15.refs_0_, bf16[1,128,1024]{2,1,0:T(8,128)(2,1)S(1)} %get-tuple-element.16.refs_1_, ...), custom_call_target="tpu_custom_call" | custom-call | tf_op jit(solution)/shard_map/pallas_call | solution.py:349

commit v6 on v5

--- a/solution.py
+++ b/solution.py
@@ -177,7 +177,7 @@
             copy1(c, ab, h).wait_recv()
         zs[0, c, ab] = (rx1[c, ab, 0] + rx1[c, ab, 1]) + (rx1[c, ab, 2] + rx1[c, ab, 3])
         exc[c, ab] = jnp.zeros_like(exc[c, ab])
-        for s in range(len(dists)):
+        for s in reversed(range(len(dists))):
             @pl.when(sends(s, ab))
             def _():
                 copyz(c, s, ab).start()

time: 28.7 us -> 28 us (0.976)
  Pallas kernels: 27.9 us -> 27.2 us
    pallas_call x1, Pallas kernels: 27 us -> 26.2 us  [local(): pl.pallas_call(functools.partial(kernel, n, ndp, rows, score_scale, facto...]
where the time goes in v6:
time: 28 us; the launch traced here: 27.8 us
  Pallas kernels  27.2 us (97%)
  between operations  0.64 us (2%)
    pallas_call x1, Pallas kernels, local(): pl.pallas_call(functools.partial(kernel, n, ndp, rows, score_scale, facto...  26.2 us
    pallas_call x1, Pallas kernels, local(): pl.pallas_call(move, out_shape=[big, big, big, small, small], in_specs=[p...  0.93 us

profile of v6, /device:TPU:0, one launch (start us, length us, event | category | flops | bytes accessed | tf_op | source)
XLA Modules:
  0.0 27.8 jit_solution(11349981547688527074)
XLA Ops:
  0.6 26.2 %shard_map.101 = (bf16[1,128,1024]{2,1,0:T(8,128)(2,1)S(1)}, bf16[1,128,1024]{2,1,0:T(8,128)(2,1)S(1)}, bf16[1,128,1024]{2,1,0:T(8,128)(2,1)S(1)}, f32[8,128]{1,0:T(8,128)S(1)}, f32[8,128]{1,0:T(8,128)S(1)}) custom-call(bf16[1,128,1024]{2,1,0:T(8,128)(2,1)} %q_h.1, bf16[1,128,1024]{2,1,0:T(8,128)(2,1)} %k_h.1, bf16[1,128,1024]{2,1,0:T(8,128)(2,1)} %v_h.1, ...), custom_call_target="tpu_custom_call" | custom-call | tf_op jit(solution)/shard_map/pallas_call | solution.py:318
  26.9 0.9 %shard_map.102 = (bf16[1,128,1024]{2,1,0:T(8,128)(2,1)}, bf16[1,128,1024]{2,1,0:T(8,128)(2,1)}, bf16[1,128,1024]{2,1,0:T(8,128)(2,1)}, f32[8,128]{1,0:T(8,128)}, f32[8,128]{1,0:T(8,128)}) custom-call(bf16[1,128,1024]{2,1,0:T(8,128)(2,1)S(1)} %get-tuple-element.15.refs_0_, bf16[1,128,1024]{2,1,0:T(8,128)(2,1)S(1)} %get-tuple-element.16.refs_1_, ...), custom_call_target="tpu_custom_call" | custom-call | tf_op jit(solution)/shard_map/pallas_call | solution.py:349
